TPU v7x, 32 devices: a whole 2x2x4 slice. The times are simulated.
32 devices in a mesh: row: 8 (over z, core), col: 4 (over y, x).
Axes of the slice: x: 2, y: 2, z: 4, core: 2. Of those that a mesh axis runs over, the one named last changes fastest.
Arguments:
- pivot_inverse: float32 [1024, 1024], P('row'), may hold values from -1 to 2, as said below
- panel: float32 [16, 1024, 1024], P('row', 'col'), may hold values from -1 to 1
- trailing: float32 [160, 1024, 1024], P('row', None, 'col'), may hold values from -6 to 6
- tile_list: int32 [160, 2], P('row'), may hold values from -1 to 15, as said below
Outputs:
- solved_panel: float32 [16, 1024, 1024], P('row', 'col')
- updated: float32 [160, 1024, 1024], P('row', None, 'col')
Inputs may be any that keep to these rules, and one draw needn't show every extreme that they name: `pivot_inverse`: lower triangular, diagonal between 0.5 and 2. `tile_list`: slots t of group g are g * 20 to g * 20 + 19. Column 0 lies in 0 to 1; column 1 is a panel tile or -1 for an empty slot. The live slots of a group come first and name distinct pairs; each group in the first half of the groups holds exactly 6 live slots, each in the second half exactly 20. Empty slots hold 0 in column 0.
All inputs are finite; a program needn't handle non-finite values.
Results may differ from a plain program's by a relative error of at most 0.00007.
Values sent between devices are 32-bit elements; how exact they have to be, the bound alone decides.
A program may use at most 128 MiB of HBM per device.

v0:
```python
import jax
import jax.numpy as jnp
from jax import lax
from jax.sharding import PartitionSpec as P

highest = lax.Precision.HIGHEST


def slot_term(left_tile, right_rows):
    return jnp.einsum("ak,bk->ab", left_tile, right_rows, precision=highest)


def per_device(pivot_inverse, panel, trailing, tile_list):
    full_pivot = lax.all_gather(pivot_inverse, "row", axis=0, tiled=True)
    slice_rows = panel.shape[1]
    tile_order = panel.shape[2]
    solved = jnp.einsum("pak,jk->paj", panel, full_pivot, precision=highest)
    whole_tiles = lax.all_gather(solved, "col", axis=1, tiled=True)
    slices = lax.all_gather(solved, "row", axis=0, tiled=True)
    empty_term = jnp.zeros((tile_order, slice_rows), jnp.float32)

    def owner_slot(listed):
        return lax.cond(
            listed[1] >= 0,
            lambda: slot_term(whole_tiles[listed[0]], slices[jnp.maximum(listed[1], 0)]),
            lambda: empty_term,
        )

    updates = lax.map(owner_slot, tile_list)
    return (solved, trailing - updates)


def solution(mesh):
    placed = (P("row", None), P("row", "col", None), P("row", None, "col"), P("row", None))
    return jax.shard_map(
        per_device,
        mesh=mesh,
        in_specs=placed,
        out_specs=(P("row", "col", None), P("row", None, "col")),
        check_vma=False,
    )
```

profile of v0, /device:TPU:17, one launch (start us, length us, event | category | flops | bytes accessed | tf_op | source)
XLA Modules:
  0.0 549.2 jit_solution(17229575436404876348)
XLA Ops:
  8.0 48.8 %all-gather.4.cloned.1.call-done = f32[1024,1024]{1,0:T(8,128)} async-done(((f32[128,1024]{1,0:T(8,128)}), f32[1024,1024]{1,0:T(8,128)}) %all-gather.4.cloned.1.call-update) | async-done | bytes 4194320 | tf_op jit(solution)/shard_map/all_gather | solution.py:14
  56.8 9.6 %fusion.9 = f32[2,256,1024]{2,1,0:T(8,128)} fusion(f32[2,256,1024]{2,1,0:T(8,128)S(1)} %copy-done, f32[1024,1024]{1,0:T(8,128)} %all-gather.4.cloned.1.call-done), kind=kOutput, calls=%fused_computation.9 | convolution fusion | flops 6442450944 | bytes 8388608 | tf_op jit(solution)/shard_map/pak,jk->paj/dot_general | solution.py:17
  67.3 86.2 %all-gather.6.cloned.1.call-done = f32[2,1024,1024]{2,1,0:T(8,128)} async-done(((f32[2,256,1024]{2,1,0:T(8,128)}), f32[2,1024,1024]{2,1,0:T(8,128)}) %all-gather.6.cloned.1.call-update) | async-done | bytes 8388624 | tf_op jit(solution)/shard_map/all_gather | solution.py:18
  153.5 152.1 %all-gather.8.cloned.1.call-done = f32[16,256,1024]{2,1,0:T(8,128)} async-done(((f32[2,256,1024]{2,1,0:T(8,128)}), f32[16,256,1024]{2,1,0:T(8,128)}) %all-gather.8.cloned.1.call-update) | async-done | bytes 16777232 | tf_op jit(solution)/shard_map/all_gather | solution.py:19
  305.6 215.2 %while.10 = (s32[]{:T(128)}, f32[20,1024,256]{2,1,0:T(8,128)}, s32[20,2]{1,0:T(8,128)S(1)}, f32[2,1024,1024]{2,1,0:T(8,128)}, f32[16,256,1024]{2,1,0:T(8,128)}, /*index=5*/s32[]{:T(128)}, s32[1,1]{1,0:T(1,128)}) while((s32[]{:T(128)}, f32[20,1024,256]{2,1,0:T(8,128)}, s32[20,2]{1,0:T(8,128)S(1)}, f32[2,1024,1024]{2,1,0:T(8,128)}, ...), condition=%wide.region_3.4_spmd, body=%wide.region_0.3_spmd.sunk | while | flops 3221225472 | bytes 8389849 | solution.py:29
  306.7 8.5 %conditional.2 = (f32[1,1024,256]{2,1,0:T(8,128)S(1)}) conditional(s32[]{:T(128)} %bitcast.18, () %tuple.35, (s32[1,2]{1,0:T(1,128)S(1)}, f32[2,1024,1024]{2,1,0:T(8,128)}, f32[16,256,1024]{2,1,0:T(8,128)}) %tuple.36), branch_computations={%region_1.1_spmd, %region_2.2_spmd} | conditional | flops 3221225472 | bytes 6292042 | solution.py:23
  309.7 5.6 %fusion.3 = f32[1,1024,256]{2,1,0:T(8,128)S(1)} fusion(f32[2,1024,1024]{2,1,0:T(8,128)} %get-tuple-element.31, s32[]{:T(128)S(6)} %select_n.0, f32[16,256,1024]{2,1,0:T(8,128)} %get-tuple-element.33, s32[]{:T(128)} %bitcast.2), kind=kOutput, calls=%fused_computation.3 | convolution fusion | flops 3221225472 | bytes 6291972 | tf_op jit(solution)/shard_map/while/body/eval_jaxpr/cond/branch_1_fun/ak,bk->ab/dot_general | solution.py:10
  315.3 1.0 constant_dynamic-update-slice_fusion.2
  317.5 8.5 %conditional.2 = (f32[1,1024,256]{2,1,0:T(8,128)S(1)}) conditional(s32[]{:T(128)} %bitcast.18, () %tuple.35, (s32[1,2]{1,0:T(1,128)S(1)}, f32[2,1024,1024]{2,1,0:T(8,128)}, f32[16,256,1024]{2,1,0:T(8,128)}) %tuple.36), branch_computations={%region_1.1_spmd, %region_2.2_spmd} | conditional | flops 3221225472 | bytes 6292042 | solution.py:23
  320.5 5.6 %fusion.3 = f32[1,1024,256]{2,1,0:T(8,128)S(1)} fusion(f32[2,1024,1024]{2,1,0:T(8,128)} %get-tuple-element.31, s32[]{:T(128)S(6)} %select_n.0, f32[16,256,1024]{2,1,0:T(8,128)} %get-tuple-element.33, s32[]{:T(128)} %bitcast.2), kind=kOutput, calls=%fused_computation.3 | convolution fusion | flops 3221225472 | bytes 6291972 | tf_op jit(solution)/shard_map/while/body/eval_jaxpr/cond/branch_1_fun/ak,bk->ab/dot_general | solution.py:10
  326.0 1.0 constant_dynamic-update-slice_fusion.2
  328.2 8.6 %conditional.2 = (f32[1,1024,256]{2,1,0:T(8,128)S(1)}) conditional(s32[]{:T(128)} %bitcast.18, () %tuple.35, (s32[1,2]{1,0:T(1,128)S(1)}, f32[2,1024,1024]{2,1,0:T(8,128)}, f32[16,256,1024]{2,1,0:T(8,128)}) %tuple.36), branch_computations={%region_1.1_spmd, %region_2.2_spmd} | conditional | flops 3221225472 | bytes 6292042 | solution.py:23
  331.2 5.6 %fusion.3 = f32[1,1024,256]{2,1,0:T(8,128)S(1)} fusion(f32[2,1024,1024]{2,1,0:T(8,128)} %get-tuple-element.31, s32[]{:T(128)S(6)} %select_n.0, f32[16,256,1024]{2,1,0:T(8,128)} %get-tuple-element.33, s32[]{:T(128)} %bitcast.2), kind=kOutput, calls=%fused_computation.3 | convolution fusion | flops 3221225472 | bytes 6291972 | tf_op jit(solution)/shard_map/while/body/eval_jaxpr/cond/branch_1_fun/ak,bk->ab/dot_general | solution.py:10
  336.8 1.0 constant_dynamic-update-slice_fusion.2
  339.0 8.5 %conditional.2 = (f32[1,1024,256]{2,1,0:T(8,128)S(1)}) conditional(s32[]{:T(128)} %bitcast.18, () %tuple.35, (s32[1,2]{1,0:T(1,128)S(1)}, f32[2,1024,1024]{2,1,0:T(8,128)}, f32[16,256,1024]{2,1,0:T(8,128)}) %tuple.36), branch_computations={%region_1.1_spmd, %region_2.2_spmd} | conditional | flops 3221225472 | bytes 6292042 | solution.py:23
  342.0 5.6 %fusion.3 = f32[1,1024,256]{2,1,0:T(8,128)S(1)} fusion(f32[2,1024,1024]{2,1,0:T(8,128)} %get-tuple-element.31, s32[]{:T(128)S(6)} %select_n.0, f32[16,256,1024]{2,1,0:T(8,128)} %get-tuple-element.33, s32[]{:T(128)} %bitcast.2), kind=kOutput, calls=%fused_computation.3 | convolution fusion | flops 3221225472 | bytes 6291972 | tf_op jit(solution)/shard_map/while/body/eval_jaxpr/cond/branch_1_fun/ak,bk->ab/dot_general | solution.py:10
  347.6 1.0 constant_dynamic-update-slice_fusion.2
  349.8 8.6 %conditional.2 = (f32[1,1024,256]{2,1,0:T(8,128)S(1)}) conditional(s32[]{:T(128)} %bitcast.18, () %tuple.35, (s32[1,2]{1,0:T(1,128)S(1)}, f32[2,1024,1024]{2,1,0:T(8,128)}, f32[16,256,1024]{2,1,0:T(8,128)}) %tuple.36), branch_computations={%region_1.1_spmd, %region_2.2_spmd} | conditional | flops 3221225472 | bytes 6292042 | solution.py:23
  352.7 5.6 %fusion.3 = f32[1,1024,256]{2,1,0:T(8,128)S(1)} fusion(f32[2,1024,1024]{2,1,0:T(8,128)} %get-tuple-element.31, s32[]{:T(128)S(6)} %select_n.0, f32[16,256,1024]{2,1,0:T(8,128)} %get-tuple-element.33, s32[]{:T(128)} %bitcast.2), kind=kOutput, calls=%fused_computation.3 | convolution fusion | flops 3221225472 | bytes 6291972 | tf_op jit(solution)/shard_map/while/body/eval_jaxpr/cond/branch_1_fun/ak,bk->ab/dot_general | solution.py:10
  358.3 1.0 constant_dynamic-update-slice_fusion.2
  360.5 8.5 %conditional.2 = (f32[1,1024,256]{2,1,0:T(8,128)S(1)}) conditional(s32[]{:T(128)} %bitcast.18, () %tuple.35, (s32[1,2]{1,0:T(1,128)S(1)}, f32[2,1024,1024]{2,1,0:T(8,128)}, f32[16,256,1024]{2,1,0:T(8,128)}) %tuple.36), branch_computations={%region_1.1_spmd, %region_2.2_spmd} | conditional | flops 3221225472 | bytes 6292042 | solution.py:23
  363.5 5.6 %fusion.3 = f32[1,1024,256]{2,1,0:T(8,128)S(1)} fusion(f32[2,1024,1024]{2,1,0:T(8,128)} %get-tuple-element.31, s32[]{:T(128)S(6)} %select_n.0, f32[16,256,1024]{2,1,0:T(8,128)} %get-tuple-element.33, s32[]{:T(128)} %bitcast.2), kind=kOutput, calls=%fused_computation.3 | convolution fusion | flops 3221225472 | bytes 6291972 | tf_op jit(solution)/shard_map/while/body/eval_jaxpr/cond/branch_1_fun/ak,bk->ab/dot_general | solution.py:10
  369.1 1.0 constant_dynamic-update-slice_fusion.2
  371.3 8.6 %conditional.2 = (f32[1,1024,256]{2,1,0:T(8,128)S(1)}) conditional(s32[]{:T(128)} %bitcast.18, () %tuple.35, (s32[1,2]{1,0:T(1,128)S(1)}, f32[2,1024,1024]{2,1,0:T(8,128)}, f32[16,256,1024]{2,1,0:T(8,128)}) %tuple.36), branch_computations={%region_1.1_spmd, %region_2.2_spmd} | conditional | flops 3221225472 | bytes 6292042 | solution.py:23
  374.2 5.6 %fusion.3 = f32[1,1024,256]{2,1,0:T(8,128)S(1)} fusion(f32[2,1024,1024]{2,1,0:T(8,128)} %get-tuple-element.31, s32[]{:T(128)S(6)} %select_n.0, f32[16,256,1024]{2,1,0:T(8,128)} %get-tuple-element.33, s32[]{:T(128)} %bitcast.2), kind=kOutput, calls=%fused_computation.3 | convolution fusion | flops 3221225472 | bytes 6291972 | tf_op jit(solution)/shard_map/while/body/eval_jaxpr/cond/branch_1_fun/ak,bk->ab/dot_general | solution.py:10
  379.8 1.0 constant_dynamic-update-slice_fusion.2
  382.0 8.5 %conditional.2 = (f32[1,1024,256]{2,1,0:T(8,128)S(1)}) conditional(s32[]{:T(128)} %bitcast.18, () %tuple.35, (s32[1,2]{1,0:T(1,128)S(1)}, f32[2,1024,1024]{2,1,0:T(8,128)}, f32[16,256,1024]{2,1,0:T(8,128)}) %tuple.36), branch_computations={%region_1.1_spmd, %region_2.2_spmd} | conditional | flops 3221225472 | bytes 6292042 | solution.py:23
  385.0 5.6 %fusion.3 = f32[1,1024,256]{2,1,0:T(8,128)S(1)} fusion(f32[2,1024,1024]{2,1,0:T(8,128)} %get-tuple-element.31, s32[]{:T(128)S(6)} %select_n.0, f32[16,256,1024]{2,1,0:T(8,128)} %get-tuple-element.33, s32[]{:T(128)} %bitcast.2), kind=kOutput, calls=%fused_computation.3 | convolution fusion | flops 3221225472 | bytes 6291972 | tf_op jit(solution)/shard_map/while/body/eval_jaxpr/cond/branch_1_fun/ak,bk->ab/dot_general | solution.py:10
  390.6 1.0 constant_dynamic-update-slice_fusion.2
  392.8 8.6 %conditional.2 = (f32[1,1024,256]{2,1,0:T(8,128)S(1)}) conditional(s32[]{:T(128)} %bitcast.18, () %tuple.35, (s32[1,2]{1,0:T(1,128)S(1)}, f32[2,1024,1024]{2,1,0:T(8,128)}, f32[16,256,1024]{2,1,0:T(8,128)}) %tuple.36), branch_computations={%region_1.1_spmd, %region_2.2_spmd} | conditional | flops 3221225472 | bytes 6292042 | solution.py:23
  395.8 5.6 %fusion.3 = f32[1,1024,256]{2,1,0:T(8,128)S(1)} fusion(f32[2,1024,1024]{2,1,0:T(8,128)} %get-tuple-element.31, s32[]{:T(128)S(6)} %select_n.0, f32[16,256,1024]{2,1,0:T(8,128)} %get-tuple-element.33, s32[]{:T(128)} %bitcast.2), kind=kOutput, calls=%fused_computation.3 | convolution fusion | flops 3221225472 | bytes 6291972 | tf_op jit(solution)/shard_map/while/body/eval_jaxpr/cond/branch_1_fun/ak,bk->ab/dot_general | solution.py:10
  401.4 1.0 constant_dynamic-update-slice_fusion.2
  403.6 8.5 %conditional.2 = (f32[1,1024,256]{2,1,0:T(8,128)S(1)}) conditional(s32[]{:T(128)} %bitcast.18, () %tuple.35, (s32[1,2]{1,0:T(1,128)S(1)}, f32[2,1024,1024]{2,1,0:T(8,128)}, f32[16,256,1024]{2,1,0:T(8,128)}) %tuple.36), branch_computations={%region_1.1_spmd, %region_2.2_spmd} | conditional | flops 3221225472 | bytes 6292042 | solution.py:23
  406.5 5.6 %fusion.3 = f32[1,1024,256]{2,1,0:T(8,128)S(1)} fusion(f32[2,1024,1024]{2,1,0:T(8,128)} %get-tuple-element.31, s32[]{:T(128)S(6)} %select_n.0, f32[16,256,1024]{2,1,0:T(8,128)} %get-tuple-element.33, s32[]{:T(128)} %bitcast.2), kind=kOutput, calls=%fused_computation.3 | convolution fusion | flops 3221225472 | bytes 6291972 | tf_op jit(solution)/shard_map/while/body/eval_jaxpr/cond/branch_1_fun/ak,bk->ab/dot_general | solution.py:10
  412.1 1.0 constant_dynamic-update-slice_fusion.2
  414.3 8.6 %conditional.2 = (f32[1,1024,256]{2,1,0:T(8,128)S(1)}) conditional(s32[]{:T(128)} %bitcast.18, () %tuple.35, (s32[1,2]{1,0:T(1,128)S(1)}, f32[2,1024,1024]{2,1,0:T(8,128)}, f32[16,256,1024]{2,1,0:T(8,128)}) %tuple.36), branch_computations={%region_1.1_spmd, %region_2.2_spmd} | conditional | flops 3221225472 | bytes 6292042 | solution.py:23
  417.3 5.6 %fusion.3 = f32[1,1024,256]{2,1,0:T(8,128)S(1)} fusion(f32[2,1024,1024]{2,1,0:T(8,128)} %get-tuple-element.31, s32[]{:T(128)S(6)} %select_n.0, f32[16,256,1024]{2,1,0:T(8,128)} %get-tuple-element.33, s32[]{:T(128)} %bitcast.2), kind=kOutput, calls=%fused_computation.3 | convolution fusion | flops 3221225472 | bytes 6291972 | tf_op jit(solution)/shard_map/while/body/eval_jaxpr/cond/branch_1_fun/ak,bk->ab/dot_general | solution.py:10
  422.9 1.0 constant_dynamic-update-slice_fusion.2
  425.1 8.5 %conditional.2 = (f32[1,1024,256]{2,1,0:T(8,128)S(1)}) conditional(s32[]{:T(128)} %bitcast.18, () %tuple.35, (s32[1,2]{1,0:T(1,128)S(1)}, f32[2,1024,1024]{2,1,0:T(8,128)}, f32[16,256,1024]{2,1,0:T(8,128)}) %tuple.36), branch_computations={%region_1.1_spmd, %region_2.2_spmd} | conditional | flops 3221225472 | bytes 6292042 | solution.py:23
  428.0 5.6 %fusion.3 = f32[1,1024,256]{2,1,0:T(8,128)S(1)} fusion(f32[2,1024,1024]{2,1,0:T(8,128)} %get-tuple-element.31, s32[]{:T(128)S(6)} %select_n.0, f32[16,256,1024]{2,1,0:T(8,128)} %get-tuple-element.33, s32[]{:T(128)} %bitcast.2), kind=kOutput, calls=%fused_computation.3 | convolution fusion | flops 3221225472 | bytes 6291972 | tf_op jit(solution)/shard_map/while/body/eval_jaxpr/cond/branch_1_fun/ak,bk->ab/dot_general | solution.py:10
  433.6 1.0 constant_dynamic-update-slice_fusion.2
  435.8 8.6 %conditional.2 = (f32[1,1024,256]{2,1,0:T(8,128)S(1)}) conditional(s32[]{:T(128)} %bitcast.18, () %tuple.35, (s32[1,2]{1,0:T(1,128)S(1)}, f32[2,1024,1024]{2,1,0:T(8,128)}, f32[16,256,1024]{2,1,0:T(8,128)}) %tuple.36), branch_computations={%region_1.1_spmd, %region_2.2_spmd} | conditional | flops 3221225472 | bytes 6292042 | solution.py:23
  438.8 5.6 %fusion.3 = f32[1,1024,256]{2,1,0:T(8,128)S(1)} fusion(f32[2,1024,1024]{2,1,0:T(8,128)} %get-tuple-element.31, s32[]{:T(128)S(6)} %select_n.0, f32[16,256,1024]{2,1,0:T(8,128)} %get-tuple-element.33, s32[]{:T(128)} %bitcast.2), kind=kOutput, calls=%fused_computation.3 | convolution fusion | flops 3221225472 | bytes 6291972 | tf_op jit(solution)/shard_map/while/body/eval_jaxpr/cond/branch_1_fun/ak,bk->ab/dot_general | solution.py:10
  444.4 1.0 constant_dynamic-update-slice_fusion.2
  446.6 8.5 %conditional.2 = (f32[1,1024,256]{2,1,0:T(8,128)S(1)}) conditional(s32[]{:T(128)} %bitcast.18, () %tuple.35, (s32[1,2]{1,0:T(1,128)S(1)}, f32[2,1024,1024]{2,1,0:T(8,128)}, f32[16,256,1024]{2,1,0:T(8,128)}) %tuple.36), branch_computations={%region_1.1_spmd, %region_2.2_spmd} | conditional | flops 3221225472 | bytes 6292042 | solution.py:23
  449.6 5.6 %fusion.3 = f32[1,1024,256]{2,1,0:T(8,128)S(1)} fusion(f32[2,1024,1024]{2,1,0:T(8,128)} %get-tuple-element.31, s32[]{:T(128)S(6)} %select_n.0, f32[16,256,1024]{2,1,0:T(8,128)} %get-tuple-element.33, s32[]{:T(128)} %bitcast.2), kind=kOutput, calls=%fused_computation.3 | convolution fusion | flops 3221225472 | bytes 6291972 | tf_op jit(solution)/shard_map/while/body/eval_jaxpr/cond/branch_1_fun/ak,bk->ab/dot_general | solution.py:10
  455.1 1.0 constant_dynamic-update-slice_fusion.2
  457.3 8.6 %conditional.2 = (f32[1,1024,256]{2,1,0:T(8,128)S(1)}) conditional(s32[]{:T(128)} %bitcast.18, () %tuple.35, (s32[1,2]{1,0:T(1,128)S(1)}, f32[2,1024,1024]{2,1,0:T(8,128)}, f32[16,256,1024]{2,1,0:T(8,128)}) %tuple.36), branch_computations={%region_1.1_spmd, %region_2.2_spmd} | conditional | flops 3221225472 | bytes 6292042 | solution.py:23
  460.3 5.6 %fusion.3 = f32[1,1024,256]{2,1,0:T(8,128)S(1)} fusion(f32[2,1024,1024]{2,1,0:T(8,128)} %get-tuple-element.31, s32[]{:T(128)S(6)} %select_n.0, f32[16,256,1024]{2,1,0:T(8,128)} %get-tuple-element.33, s32[]{:T(128)} %bitcast.2), kind=kOutput, calls=%fused_computation.3 | convolution fusion | flops 3221225472 | bytes 6291972 | tf_op jit(solution)/shard_map/while/body/eval_jaxpr/cond/branch_1_fun/ak,bk->ab/dot_general | solution.py:10
  465.9 1.0 constant_dynamic-update-slice_fusion.2
  468.1 8.5 %conditional.2 = (f32[1,1024,256]{2,1,0:T(8,128)S(1)}) conditional(s32[]{:T(128)} %bitcast.18, () %tuple.35, (s32[1,2]{1,0:T(1,128)S(1)}, f32[2,1024,1024]{2,1,0:T(8,128)}, f32[16,256,1024]{2,1,0:T(8,128)}) %tuple.36), branch_computations={%region_1.1_spmd, %region_2.2_spmd} | conditional | flops 3221225472 | bytes 6292042 | solution.py:23
  471.1 5.6 %fusion.3 = f32[1,1024,256]{2,1,0:T(8,128)S(1)} fusion(f32[2,1024,1024]{2,1,0:T(8,128)} %get-tuple-element.31, s32[]{:T(128)S(6)} %select_n.0, f32[16,256,1024]{2,1,0:T(8,128)} %get-tuple-element.33, s32[]{:T(128)} %bitcast.2), kind=kOutput, calls=%fused_computation.3 | convolution fusion | flops 3221225472 | bytes 6291972 | tf_op jit(solution)/shard_map/while/body/eval_jaxpr/cond/branch_1_fun/ak,bk->ab/dot_general | solution.py:10
  476.7 1.0 constant_dynamic-update-slice_fusion.2
  478.9 8.6 %conditional.2 = (f32[1,1024,256]{2,1,0:T(8,128)S(1)}) conditional(s32[]{:T(128)} %bitcast.18, () %tuple.35, (s32[1,2]{1,0:T(1,128)S(1)}, f32[2,1024,1024]{2,1,0:T(8,128)}, f32[16,256,1024]{2,1,0:T(8,128)}) %tuple.36), branch_computations={%region_1.1_spmd, %region_2.2_spmd} | conditional | flops 3221225472 | bytes 6292042 | solution.py:23
  481.8 5.6 %fusion.3 = f32[1,1024,256]{2,1,0:T(8,128)S(1)} fusion(f32[2,1024,1024]{2,1,0:T(8,128)} %get-tuple-element.31, s32[]{:T(128)S(6)} %select_n.0, f32[16,256,1024]{2,1,0:T(8,128)} %get-tuple-element.33, s32[]{:T(128)} %bitcast.2), kind=kOutput, calls=%fused_computation.3 | convolution fusion | flops 3221225472 | bytes 6291972 | tf_op jit(solution)/shard_map/while/body/eval_jaxpr/cond/branch_1_fun/ak,bk->ab/dot_general | solution.py:10
  487.4 1.0 constant_dynamic-update-slice_fusion.2
  489.6 8.5 %conditional.2 = (f32[1,1024,256]{2,1,0:T(8,128)S(1)}) conditional(s32[]{:T(128)} %bitcast.18, () %tuple.35, (s32[1,2]{1,0:T(1,128)S(1)}, f32[2,1024,1024]{2,1,0:T(8,128)}, f32[16,256,1024]{2,1,0:T(8,128)}) %tuple.36), branch_computations={%region_1.1_spmd, %region_2.2_spmd} | conditional | flops 3221225472 | bytes 6292042 | solution.py:23
  492.6 5.6 %fusion.3 = f32[1,1024,256]{2,1,0:T(8,128)S(1)} fusion(f32[2,1024,1024]{2,1,0:T(8,128)} %get-tuple-element.31, s32[]{:T(128)S(6)} %select_n.0, f32[16,256,1024]{2,1,0:T(8,128)} %get-tuple-element.33, s32[]{:T(128)} %bitcast.2), kind=kOutput, calls=%fused_computation.3 | convolution fusion | flops 3221225472 | bytes 6291972 | tf_op jit(solution)/shard_map/while/body/eval_jaxpr/cond/branch_1_fun/ak,bk->ab/dot_general | solution.py:10
  498.2 1.0 constant_dynamic-update-slice_fusion.2
  500.4 8.6 %conditional.2 = (f32[1,1024,256]{2,1,0:T(8,128)S(1)}) conditional(s32[]{:T(128)} %bitcast.18, () %tuple.35, (s32[1,2]{1,0:T(1,128)S(1)}, f32[2,1024,1024]{2,1,0:T(8,128)}, f32[16,256,1024]{2,1,0:T(8,128)}) %tuple.36), branch_computations={%region_1.1_spmd, %region_2.2_spmd} | conditional | flops 3221225472 | bytes 6292042 | solution.py:23
  503.3 5.6 %fusion.3 = f32[1,1024,256]{2,1,0:T(8,128)S(1)} fusion(f32[2,1024,1024]{2,1,0:T(8,128)} %get-tuple-element.31, s32[]{:T(128)S(6)} %select_n.0, f32[16,256,1024]{2,1,0:T(8,128)} %get-tuple-element.33, s32[]{:T(128)} %bitcast.2), kind=kOutput, calls=%fused_computation.3 | convolution fusion | flops 3221225472 | bytes 6291972 | tf_op jit(solution)/shard_map/while/body/eval_jaxpr/cond/branch_1_fun/ak,bk->ab/dot_general | solution.py:10
  511.1 8.5 %conditional.2 = (f32[1,1024,256]{2,1,0:T(8,128)S(1)}) conditional(s32[]{:T(128)} %bitcast.18, () %tuple.35, (s32[1,2]{1,0:T(1,128)S(1)}, f32[2,1024,1024]{2,1,0:T(8,128)}, f32[16,256,1024]{2,1,0:T(8,128)}) %tuple.36), branch_computations={%region_1.1_spmd, %region_2.2_spmd} | conditional | flops 3221225472 | bytes 6292042 | solution.py:23
  514.1 5.6 %fusion.3 = f32[1,1024,256]{2,1,0:T(8,128)S(1)} fusion(f32[2,1024,1024]{2,1,0:T(8,128)} %get-tuple-element.31, s32[]{:T(128)S(6)} %select_n.0, f32[16,256,1024]{2,1,0:T(8,128)} %get-tuple-element.33, s32[]{:T(128)} %bitcast.2), kind=kOutput, calls=%fused_computation.3 | convolution fusion | flops 3221225472 | bytes 6291972 | tf_op jit(solution)/shard_map/while/body/eval_jaxpr/cond/branch_1_fun/ak,bk->ab/dot_general | solution.py:10
  520.7 21.9 %sub.3 = f32[20,1024,256]{2,1,0:T(8,128)} subtract(f32[20,1024,256]{2,1,0:T(8,128)} %param.10, f32[20,1024,256]{2,1,0:T(8,128)} %get-tuple-element.43) | non-fusion elementwise | flops 5242880 | bytes 62914560 | tf_op jit(solution)/shard_map/sub | solution.py:30
  (76 shorter events, 27.5 us)
Async XLA Ops:
  7.2 49.6 %copy-start = (f32[2,256,1024]{2,1,0:T(8,128)S(1)}, f32[2,256,1024]{2,1,0:T(8,128)}, u32[]{:S(2)}) copy-start(f32[2,256,1024]{2,1,0:T(8,128)} %param.9) | copy-start | bytes 6291460
  7.2 60.0 %copy-start.2 = (s32[20,2]{0,1:T(2,128)S(1)}, s32[20,2]{0,1:T(2,128)}, u32[]{:S(2)}) copy-start(s32[20,2]{0,1:T(2,128)} %param.11) | copy-start | bytes 484
  7.2 49.6 %all-gather.4.cloned.1.call-start = ((), (), s32[]{:S(2)}) async-start(), calls=%async_computation | async-start | bytes 4718592 | tf_op jit(solution)/shard_map/all_gather | solution.py:14
  7.9 145.6 %all-gather.6.cloned.1.call-start = ((), (), s32[]{:S(2)}) async-start(), calls=%async_computation.1 | async-start | bytes 10485760 | tf_op jit(solution)/shard_map/all_gather | solution.py:18
  66.4 239.1 %all-gather.8.cloned.1.call-start = ((), (), s32[]{:S(2)}) async-start(), calls=%async_computation.2 | async-start | bytes 18874368 | tf_op jit(solution)/shard_map/all_gather | solution.py:19
  520.7 21.9 %copy-start.1 = (f32[2,256,1024]{2,1,0:T(8,128)S(1)}, f32[2,256,1024]{2,1,0:T(8,128)}, u32[]{:S(2)}) copy-start(f32[2,256,1024]{2,1,0:T(8,128)} %param.9) | copy-start | bytes 6291460
Sparse Core Ops, SparseCore 0:
  9.6 47.1 all-gather.3
  66.6 86.8 all-gather.5
  155.7 149.8 all-gather.7
where the time goes:
time: 550 us; the launch traced here: 549 us
  waiting for transfers between devices  288 us (52%)
  matrix products  121 us (22%)
  loops' own time  59 us (11%)
  local copies, waits for them, and re-layouts  44.7 us (8%)
  other arithmetic  21.9 us (4%)
  between operations  13.8 us (3%)
    all_gather x1, waiting for transfers between devices, per_device(): slices = lax.all_gather(solved, 'row', axis=0, tiled=True)  152 us
    dot_general x20, matrix products, slot_term(): return jnp.einsum('ak,bk->ab', left_tile, right_rows, precision=highest)  112 us
    all_gather x1, waiting for transfers between devices, per_device(): whole_tiles = lax.all_gather(solved, 'col', axis=1, tiled=True)  86.2 us
    all_gather x1, waiting for transfers between devices, per_device(): full_pivot = lax.all_gather(pivot_inverse, 'row', axis=0, tiled=True)  48.8 us
    another operation x20, loops' own time, owner_slot(): lax.cond(listed[1] >= 0, lambda: slot_term(whole_tiles[listed[0]], slices...  47.3 us
    sub x1, other arithmetic, per_device(): return (solved, trailing - updates)  21.9 us
    dynamic_update_slice x20, local copies, waits for them, and re-layouts, per_device(): updates = lax.map(owner_slot, tile_list)  20.9 us
    slice x20, local copies, waits for them, and re-layouts, owner_slot(): listed[1]  12.1 us
  transfers between devices with their start and end apart: 3, of which 3 were waited for; matrix products, arithmetic and copies ran while one was open for 0% of the time, Pallas kernels for 0%

commit v1 on v0

--- a/solution.py
+++ b/solution.py
@@ -15,7 +15,12 @@
     slice_rows = panel.shape[1]
     tile_order = panel.shape[2]
     solved = jnp.einsum("pak,jk->paj", panel, full_pivot, precision=highest)
-    whole_tiles = lax.all_gather(solved, "col", axis=1, tiled=True)
+    ring = [solved]
+    for hop in range(3):
+        ring.append(lax.ppermute(ring[-1], "col", [(dev, (dev + 1) % 4) for dev in range(4)]))
+    whole_tiles = jnp.roll(
+        jnp.concatenate(ring[::-1], axis=1), (lax.axis_index("col") + 1) * ring[0].shape[1], axis=1
+    )
     slices = lax.all_gather(solved, "row", axis=0, tiled=True)
     empty_term = jnp.zeros((tile_order, slice_rows), jnp.float32)
 

time: 550 us -> 476 us (0.87)
  waiting for transfers between devices: 288 us -> 189 us
  local copies, waits for them, and re-layouts: 44.7 us -> 62 us
    all_gather x1, waiting for transfers between devices: 152 us -> 0.01 us  [per_device(): slices = lax.all_gather(solved, 'row', axis=0, tiled=True)]
    ppermute x0 -> x3, waiting for transfers between devices: none -> 140 us  [per_device(): lax.ppermute(ring[-1], 'col', [(dev, (dev + 1) % 4) for dev in range(4)])]
    all_gather x1 -> x0, waiting for transfers between devices: 86.2 us -> none  [per_device(): whole_tiles = lax.all_gather(solved, 'col', axis=1, tiled=True)]
    unnamed x6 -> x17, local copies, waits for them, and re-layouts: 0.02 us -> 12 us
  transfers between devices with their start and end apart: 3 -> 5, of which waited for: 3 -> 4; matrix products, arithmetic and copies ran while one was open for 0% -> 3% of each run, Pallas kernels for 0% -> 0%
where the time goes in v1:
time: 476 us; the launch traced here: 473 us
  waiting for transfers between devices  189 us (40%)
  matrix products  121 us (25%)
  loops' own time  62.7 us (13%)
  local copies, waits for them, and re-layouts  62 us (13%)
  other arithmetic  21.9 us (5%)
  between operations  14.1 us (3%)
    ppermute x3, waiting for transfers between devices, per_device(): lax.ppermute(ring[-1], 'col', [(dev, (dev + 1) % 4) for dev in range(4)])  140 us
    dot_general x20, matrix products, slot_term(): return jnp.einsum('ak,bk->ab', left_tile, right_rows, precision=highest)  111 us
    another operation x20, loops' own time, owner_slot(): lax.cond(listed[1] >= 0, lambda: slot_term(whole_tiles[listed[0]], slices...  51 us
    all_gather x1, waiting for transfers between devices, per_device(): full_pivot = lax.all_gather(pivot_inverse, 'row', axis=0, tiled=True)  48.8 us
    sub x1, other arithmetic, per_device(): return (solved, trailing - updates)  21.9 us
    dynamic_update_slice x20, local copies, waits for them, and re-layouts, per_device(): updates = lax.map(owner_slot, tile_list)  20.9 us
    slice x20, local copies, waits for them, and re-layouts, owner_slot(): listed[1]  12.9 us
    unnamed x17, local copies, waits for them, and re-layouts  12 us
  transfers between devices with their start and end apart: 5, of which 4 were waited for; matrix products, arithmetic and copies ran while one was open for 3% of the time, Pallas kernels for 0%

profile of v1, /device:TPU:17, one launch (start us, length us, event | category | flops | bytes accessed | tf_op | source)
XLA Modules:
  0.0 472.5 jit_solution(3996418594309815739)
XLA Ops:
  8.0 48.8 %all-gather.3.cloned.1.call-done = f32[1024,1024]{1,0:T(8,128)} async-done(((f32[128,1024]{1,0:T(8,128)}), f32[1024,1024]{1,0:T(8,128)}) %all-gather.3.cloned.1.call-update) | async-done | bytes 4194320 | tf_op jit(solution)/shard_map/all_gather | solution.py:14
  56.8 9.6 %fusion.9 = f32[2,256,1024]{2,1,0:T(8,128)} fusion(f32[2,256,1024]{2,1,0:T(8,128)S(1)} %copy-done, f32[1024,1024]{1,0:T(8,128)} %all-gather.3.cloned.1.call-done), kind=kOutput, calls=%fused_computation.9 | convolution fusion | flops 6442450944 | bytes 8388608 | tf_op jit(solution)/shard_map/pak,jk->paj/dot_general | solution.py:17
  66.4 1.2 collective-permute-start
  67.7 46.9 %collective-permute-done = f32[2,256,1024]{2,1,0:T(8,128)S(1)} collective-permute-done((f32[2,256,1024]{2,1,0:T(8,128)}, f32[2,256,1024]{2,1,0:T(8,128)S(1)}, u32[]{:S(2)}, u32[]{:S(2)}) %collective-permute-start) | collective-permute-done | bytes 2097184 | tf_op jit(solution)/shard_map/ppermute | solution.py:20
  114.6 1.3 copy-done.3
  116.2 46.9 %collective-permute-done.1 = f32[2,256,1024]{2,1,0:T(8,128)} collective-permute-done((f32[2,256,1024]{2,1,0:T(8,128)S(1)}, f32[2,256,1024]{2,1,0:T(8,128)}, u32[]{:S(2)}, u32[]{:S(2)}) %collective-permute-start.1) | collective-permute-done | bytes 2097184 | tf_op jit(solution)/shard_map/ppermute | solution.py:20
  163.9 45.7 %collective-permute-done.2 = f32[2,256,1024]{2,1,0:T(8,128)} collective-permute-done((f32[2,256,1024]{2,1,0:T(8,128)}, f32[2,256,1024]{2,1,0:T(8,128)}, u32[]{:S(2)}, u32[]{:S(2)}) %collective-permute-start.2) | collective-permute-done | bytes 2097184 | tf_op jit(solution)/shard_map/ppermute | solution.py:20
  209.6 1.7 constant_dynamic-update-slice_fusion.8
  211.4 1.7 constant_dynamic-update-slice_fusion.7
  213.1 1.7 constant_dynamic-update-slice_fusion.6
  214.8 1.7 constant_dynamic-update-slice_fusion.5
  216.6 1.7 constant_dynamic-update-slice_fusion.4
  218.3 1.7 constant_dynamic-update-slice_fusion.3
  220.4 4.1 constant_dynamic-slice_fusion.1
  224.5 219.2 %while.10 = (s32[]{:T(128)}, f32[20,1024,256]{2,1,0:T(8,128)}, s32[20,2]{1,0:T(8,128)S(1)}, f32[2,1024,1024]{2,1,0:T(8,128)}, f32[16,256,1024]{2,1,0:T(8,128)}, /*index=5*/s32[]{:T(128)}, s32[1,1]{1,0:T(1,128)}) while((s32[]{:T(128)}, f32[20,1024,256]{2,1,0:T(8,128)}, s32[20,2]{1,0:T(8,128)S(1)}, f32[2,1024,1024]{2,1,0:T(8,128)}, ...), condition=%wide.region_3.4_spmd, body=%wide.region_0.3_spmd.sunk | while | flops 3221225472 | bytes 8389849 | solution.py:34
  225.7 8.8 %conditional.2 = (f32[1,1024,256]{2,1,0:T(8,128)S(1)}) conditional(s32[]{:T(128)} %bitcast.18, () %tuple.35, (s32[1,2]{1,0:T(1,128)S(1)}, f32[2,1024,1024]{2,1,0:T(8,128)}, f32[16,256,1024]{2,1,0:T(8,128)}) %tuple.36), branch_computations={%region_1.1_spmd, %region_2.2_spmd} | conditional | flops 3221225472 | bytes 6292042 | solution.py:28
  228.9 5.6 %fusion.3 = f32[1,1024,256]{2,1,0:T(8,128)S(1)} fusion(f32[2,1024,1024]{2,1,0:T(8,128)} %get-tuple-element.31, s32[]{:T(128)S(6)} %select_n.14, f32[16,256,1024]{2,1,0:T(8,128)} %get-tuple-element.33, s32[]{:T(128)} %bitcast.2), kind=kOutput, calls=%fused_computation.3 | convolution fusion | flops 3221225472 | bytes 6291972 | tf_op jit(solution)/shard_map/while/body/eval_jaxpr/cond/branch_1_fun/ak,bk->ab/dot_general | solution.py:10
  234.5 1.0 constant_dynamic-update-slice_fusion.10
  236.6 8.8 %conditional.2 = (f32[1,1024,256]{2,1,0:T(8,128)S(1)}) conditional(s32[]{:T(128)} %bitcast.18, () %tuple.35, (s32[1,2]{1,0:T(1,128)S(1)}, f32[2,1024,1024]{2,1,0:T(8,128)}, f32[16,256,1024]{2,1,0:T(8,128)}) %tuple.36), branch_computations={%region_1.1_spmd, %region_2.2_spmd} | conditional | flops 3221225472 | bytes 6292042 | solution.py:28
  239.8 5.6 %fusion.3 = f32[1,1024,256]{2,1,0:T(8,128)S(1)} fusion(f32[2,1024,1024]{2,1,0:T(8,128)} %get-tuple-element.31, s32[]{:T(128)S(6)} %select_n.14, f32[16,256,1024]{2,1,0:T(8,128)} %get-tuple-element.33, s32[]{:T(128)} %bitcast.2), kind=kOutput, calls=%fused_computation.3 | convolution fusion | flops 3221225472 | bytes 6291972 | tf_op jit(solution)/shard_map/while/body/eval_jaxpr/cond/branch_1_fun/ak,bk->ab/dot_general | solution.py:10
  245.4 1.0 constant_dynamic-update-slice_fusion.10
  247.6 8.8 %conditional.2 = (f32[1,1024,256]{2,1,0:T(8,128)S(1)}) conditional(s32[]{:T(128)} %bitcast.18, () %tuple.35, (s32[1,2]{1,0:T(1,128)S(1)}, f32[2,1024,1024]{2,1,0:T(8,128)}, f32[16,256,1024]{2,1,0:T(8,128)}) %tuple.36), branch_computations={%region_1.1_spmd, %region_2.2_spmd} | conditional | flops 3221225472 | bytes 6292042 | solution.py:28
  250.8 5.6 %fusion.3 = f32[1,1024,256]{2,1,0:T(8,128)S(1)} fusion(f32[2,1024,1024]{2,1,0:T(8,128)} %get-tuple-element.31, s32[]{:T(128)S(6)} %select_n.14, f32[16,256,1024]{2,1,0:T(8,128)} %get-tuple-element.33, s32[]{:T(128)} %bitcast.2), kind=kOutput, calls=%fused_computation.3 | convolution fusion | flops 3221225472 | bytes 6291972 | tf_op jit(solution)/shard_map/while/body/eval_jaxpr/cond/branch_1_fun/ak,bk->ab/dot_general | solution.py:10
  256.4 1.0 constant_dynamic-update-slice_fusion.10
  258.6 8.8 %conditional.2 = (f32[1,1024,256]{2,1,0:T(8,128)S(1)}) conditional(s32[]{:T(128)} %bitcast.18, () %tuple.35, (s32[1,2]{1,0:T(1,128)S(1)}, f32[2,1024,1024]{2,1,0:T(8,128)}, f32[16,256,1024]{2,1,0:T(8,128)}) %tuple.36), branch_computations={%region_1.1_spmd, %region_2.2_spmd} | conditional | flops 3221225472 | bytes 6292042 | solution.py:28
  261.8 5.6 %fusion.3 = f32[1,1024,256]{2,1,0:T(8,128)S(1)} fusion(f32[2,1024,1024]{2,1,0:T(8,128)} %get-tuple-element.31, s32[]{:T(128)S(6)} %select_n.14, f32[16,256,1024]{2,1,0:T(8,128)} %get-tuple-element.33, s32[]{:T(128)} %bitcast.2), kind=kOutput, calls=%fused_computation.3 | convolution fusion | flops 3221225472 | bytes 6291972 | tf_op jit(solution)/shard_map/while/body/eval_jaxpr/cond/branch_1_fun/ak,bk->ab/dot_general | solution.py:10
  267.3 1.0 constant_dynamic-update-slice_fusion.10
  269.5 8.8 %conditional.2 = (f32[1,1024,256]{2,1,0:T(8,128)S(1)}) conditional(s32[]{:T(128)} %bitcast.18, () %tuple.35, (s32[1,2]{1,0:T(1,128)S(1)}, f32[2,1024,1024]{2,1,0:T(8,128)}, f32[16,256,1024]{2,1,0:T(8,128)}) %tuple.36), branch_computations={%region_1.1_spmd, %region_2.2_spmd} | conditional | flops 3221225472 | bytes 6292042 | solution.py:28
  272.7 5.6 %fusion.3 = f32[1,1024,256]{2,1,0:T(8,128)S(1)} fusion(f32[2,1024,1024]{2,1,0:T(8,128)} %get-tuple-element.31, s32[]{:T(128)S(6)} %select_n.14, f32[16,256,1024]{2,1,0:T(8,128)} %get-tuple-element.33, s32[]{:T(128)} %bitcast.2), kind=kOutput, calls=%fused_computation.3 | convolution fusion | flops 3221225472 | bytes 6291972 | tf_op jit(solution)/shard_map/while/body/eval_jaxpr/cond/branch_1_fun/ak,bk->ab/dot_general | solution.py:10
  278.3 1.0 constant_dynamic-update-slice_fusion.10
  280.5 8.8 %conditional.2 = (f32[1,1024,256]{2,1,0:T(8,128)S(1)}) conditional(s32[]{:T(128)} %bitcast.18, () %tuple.35, (s32[1,2]{1,0:T(1,128)S(1)}, f32[2,1024,1024]{2,1,0:T(8,128)}, f32[16,256,1024]{2,1,0:T(8,128)}) %tuple.36), branch_computations={%region_1.1_spmd, %region_2.2_spmd} | conditional | flops 3221225472 | bytes 6292042 | solution.py:28
  283.7 5.6 %fusion.3 = f32[1,1024,256]{2,1,0:T(8,128)S(1)} fusion(f32[2,1024,1024]{2,1,0:T(8,128)} %get-tuple-element.31, s32[]{:T(128)S(6)} %select_n.14, f32[16,256,1024]{2,1,0:T(8,128)} %get-tuple-element.33, s32[]{:T(128)} %bitcast.2), kind=kOutput, calls=%fused_computation.3 | convolution fusion | flops 3221225472 | bytes 6291972 | tf_op jit(solution)/shard_map/while/body/eval_jaxpr/cond/branch_1_fun/ak,bk->ab/dot_general | solution.py:10
  289.3 1.0 constant_dynamic-update-slice_fusion.10
  291.4 8.8 %conditional.2 = (f32[1,1024,256]{2,1,0:T(8,128)S(1)}) conditional(s32[]{:T(128)} %bitcast.18, () %tuple.35, (s32[1,2]{1,0:T(1,128)S(1)}, f32[2,1024,1024]{2,1,0:T(8,128)}, f32[16,256,1024]{2,1,0:T(8,128)}) %tuple.36), branch_computations={%region_1.1_spmd, %region_2.2_spmd} | conditional | flops 3221225472 | bytes 6292042 | solution.py:28
  294.6 5.6 %fusion.3 = f32[1,1024,256]{2,1,0:T(8,128)S(1)} fusion(f32[2,1024,1024]{2,1,0:T(8,128)} %get-tuple-element.31, s32[]{:T(128)S(6)} %select_n.14, f32[16,256,1024]{2,1,0:T(8,128)} %get-tuple-element.33, s32[]{:T(128)} %bitcast.2), kind=kOutput, calls=%fused_computation.3 | convolution fusion | flops 3221225472 | bytes 6291972 | tf_op jit(solution)/shard_map/while/body/eval_jaxpr/cond/branch_1_fun/ak,bk->ab/dot_general | solution.py:10
  300.2 1.0 constant_dynamic-update-slice_fusion.10
  302.4 8.8 %conditional.2 = (f32[1,1024,256]{2,1,0:T(8,128)S(1)}) conditional(s32[]{:T(128)} %bitcast.18, () %tuple.35, (s32[1,2]{1,0:T(1,128)S(1)}, f32[2,1024,1024]{2,1,0:T(8,128)}, f32[16,256,1024]{2,1,0:T(8,128)}) %tuple.36), branch_computations={%region_1.1_spmd, %region_2.2_spmd} | conditional | flops 3221225472 | bytes 6292042 | solution.py:28
  305.6 5.6 %fusion.3 = f32[1,1024,256]{2,1,0:T(8,128)S(1)} fusion(f32[2,1024,1024]{2,1,0:T(8,128)} %get-tuple-element.31, s32[]{:T(128)S(6)} %select_n.14, f32[16,256,1024]{2,1,0:T(8,128)} %get-tuple-element.33, s32[]{:T(128)} %bitcast.2), kind=kOutput, calls=%fused_computation.3 | convolution fusion | flops 3221225472 | bytes 6291972 | tf_op jit(solution)/shard_map/while/body/eval_jaxpr/cond/branch_1_fun/ak,bk->ab/dot_general | solution.py:10
  313.4 8.8 %conditional.2 = (f32[1,1024,256]{2,1,0:T(8,128)S(1)}) conditional(s32[]{:T(128)} %bitcast.18, () %tuple.35, (s32[1,2]{1,0:T(1,128)S(1)}, f32[2,1024,1024]{2,1,0:T(8,128)}, f32[16,256,1024]{2,1,0:T(8,128)}) %tuple.36), branch_computations={%region_1.1_spmd, %region_2.2_spmd} | conditional | flops 3221225472 | bytes 6292042 | solution.py:28
  316.6 5.6 %fusion.3 = f32[1,1024,256]{2,1,0:T(8,128)S(1)} fusion(f32[2,1024,1024]{2,1,0:T(8,128)} %get-tuple-element.31, s32[]{:T(128)S(6)} %select_n.14, f32[16,256,1024]{2,1,0:T(8,128)} %get-tuple-element.33, s32[]{:T(128)} %bitcast.2), kind=kOutput, calls=%fused_computation.3 | convolution fusion | flops 3221225472 | bytes 6291972 | tf_op jit(solution)/shard_map/while/body/eval_jaxpr/cond/branch_1_fun/ak,bk->ab/dot_general | solution.py:10
  324.3 8.8 %conditional.2 = (f32[1,1024,256]{2,1,0:T(8,128)S(1)}) conditional(s32[]{:T(128)} %bitcast.18, () %tuple.35, (s32[1,2]{1,0:T(1,128)S(1)}, f32[2,1024,1024]{2,1,0:T(8,128)}, f32[16,256,1024]{2,1,0:T(8,128)}) %tuple.36), branch_computations={%region_1.1_spmd, %region_2.2_spmd} | conditional | flops 3221225472 | bytes 6292042 | solution.py:28
  327.5 5.6 %fusion.3 = f32[1,1024,256]{2,1,0:T(8,128)S(1)} fusion(f32[2,1024,1024]{2,1,0:T(8,128)} %get-tuple-element.31, s32[]{:T(128)S(6)} %select_n.14, f32[16,256,1024]{2,1,0:T(8,128)} %get-tuple-element.33, s32[]{:T(128)} %bitcast.2), kind=kOutput, calls=%fused_computation.3 | convolution fusion | flops 3221225472 | bytes 6291972 | tf_op jit(solution)/shard_map/while/body/eval_jaxpr/cond/branch_1_fun/ak,bk->ab/dot_general | solution.py:10
  335.3 8.8 %conditional.2 = (f32[1,1024,256]{2,1,0:T(8,128)S(1)}) conditional(s32[]{:T(128)} %bitcast.18, () %tuple.35, (s32[1,2]{1,0:T(1,128)S(1)}, f32[2,1024,1024]{2,1,0:T(8,128)}, f32[16,256,1024]{2,1,0:T(8,128)}) %tuple.36), branch_computations={%region_1.1_spmd, %region_2.2_spmd} | conditional | flops 3221225472 | bytes 6292042 | solution.py:28
  338.5 5.6 %fusion.3 = f32[1,1024,256]{2,1,0:T(8,128)S(1)} fusion(f32[2,1024,1024]{2,1,0:T(8,128)} %get-tuple-element.31, s32[]{:T(128)S(6)} %select_n.14, f32[16,256,1024]{2,1,0:T(8,128)} %get-tuple-element.33, s32[]{:T(128)} %bitcast.2), kind=kOutput, calls=%fused_computation.3 | convolution fusion | flops 3221225472 | bytes 6291972 | tf_op jit(solution)/shard_map/while/body/eval_jaxpr/cond/branch_1_fun/ak,bk->ab/dot_general | solution.py:10
  346.2 8.8 %conditional.2 = (f32[1,1024,256]{2,1,0:T(8,128)S(1)}) conditional(s32[]{:T(128)} %bitcast.18, () %tuple.35, (s32[1,2]{1,0:T(1,128)S(1)}, f32[2,1024,1024]{2,1,0:T(8,128)}, f32[16,256,1024]{2,1,0:T(8,128)}) %tuple.36), branch_computations={%region_1.1_spmd, %region_2.2_spmd} | conditional | flops 3221225472 | bytes 6292042 | solution.py:28
  349.4 5.6 %fusion.3 = f32[1,1024,256]{2,1,0:T(8,128)S(1)} fusion(f32[2,1024,1024]{2,1,0:T(8,128)} %get-tuple-element.31, s32[]{:T(128)S(6)} %select_n.14, f32[16,256,1024]{2,1,0:T(8,128)} %get-tuple-element.33, s32[]{:T(128)} %bitcast.2), kind=kOutput, calls=%fused_computation.3 | convolution fusion | flops 3221225472 | bytes 6291972 | tf_op jit(solution)/shard_map/while/body/eval_jaxpr/cond/branch_1_fun/ak,bk->ab/dot_general | solution.py:10
  355.0 1.0 constant_dynamic-update-slice_fusion.10
  357.2 8.8 %conditional.2 = (f32[1,1024,256]{2,1,0:T(8,128)S(1)}) conditional(s32[]{:T(128)} %bitcast.18, () %tuple.35, (s32[1,2]{1,0:T(1,128)S(1)}, f32[2,1024,1024]{2,1,0:T(8,128)}, f32[16,256,1024]{2,1,0:T(8,128)}) %tuple.36), branch_computations={%region_1.1_spmd, %region_2.2_spmd} | conditional | flops 3221225472 | bytes 6292042 | solution.py:28
  360.4 5.6 %fusion.3 = f32[1,1024,256]{2,1,0:T(8,128)S(1)} fusion(f32[2,1024,1024]{2,1,0:T(8,128)} %get-tuple-element.31, s32[]{:T(128)S(6)} %select_n.14, f32[16,256,1024]{2,1,0:T(8,128)} %get-tuple-element.33, s32[]{:T(128)} %bitcast.2), kind=kOutput, calls=%fused_computation.3 | convolution fusion | flops 3221225472 | bytes 6291972 | tf_op jit(solution)/shard_map/while/body/eval_jaxpr/cond/branch_1_fun/ak,bk->ab/dot_general | solution.py:10
  368.2 8.8 %conditional.2 = (f32[1,1024,256]{2,1,0:T(8,128)S(1)}) conditional(s32[]{:T(128)} %bitcast.18, () %tuple.35, (s32[1,2]{1,0:T(1,128)S(1)}, f32[2,1024,1024]{2,1,0:T(8,128)}, f32[16,256,1024]{2,1,0:T(8,128)}) %tuple.36), branch_computations={%region_1.1_spmd, %region_2.2_spmd} | conditional | flops 3221225472 | bytes 6292042 | solution.py:28
  371.4 5.6 %fusion.3 = f32[1,1024,256]{2,1,0:T(8,128)S(1)} fusion(f32[2,1024,1024]{2,1,0:T(8,128)} %get-tuple-element.31, s32[]{:T(128)S(6)} %select_n.14, f32[16,256,1024]{2,1,0:T(8,128)} %get-tuple-element.33, s32[]{:T(128)} %bitcast.2), kind=kOutput, calls=%fused_computation.3 | convolution fusion | flops 3221225472 | bytes 6291972 | tf_op jit(solution)/shard_map/while/body/eval_jaxpr/cond/branch_1_fun/ak,bk->ab/dot_general | solution.py:10
  379.1 8.8 %conditional.2 = (f32[1,1024,256]{2,1,0:T(8,128)S(1)}) conditional(s32[]{:T(128)} %bitcast.18, () %tuple.35, (s32[1,2]{1,0:T(1,128)S(1)}, f32[2,1024,1024]{2,1,0:T(8,128)}, f32[16,256,1024]{2,1,0:T(8,128)}) %tuple.36), branch_computations={%region_1.1_spmd, %region_2.2_spmd} | conditional | flops 3221225472 | bytes 6292042 | solution.py:28
  382.3 5.6 %fusion.3 = f32[1,1024,256]{2,1,0:T(8,128)S(1)} fusion(f32[2,1024,1024]{2,1,0:T(8,128)} %get-tuple-element.31, s32[]{:T(128)S(6)} %select_n.14, f32[16,256,1024]{2,1,0:T(8,128)} %get-tuple-element.33, s32[]{:T(128)} %bitcast.2), kind=kOutput, calls=%fused_computation.3 | convolution fusion | flops 3221225472 | bytes 6291972 | tf_op jit(solution)/shard_map/while/body/eval_jaxpr/cond/branch_1_fun/ak,bk->ab/dot_general | solution.py:10
  390.1 8.8 %conditional.2 = (f32[1,1024,256]{2,1,0:T(8,128)S(1)}) conditional(s32[]{:T(128)} %bitcast.18, () %tuple.35, (s32[1,2]{1,0:T(1,128)S(1)}, f32[2,1024,1024]{2,1,0:T(8,128)}, f32[16,256,1024]{2,1,0:T(8,128)}) %tuple.36), branch_computations={%region_1.1_spmd, %region_2.2_spmd} | conditional | flops 3221225472 | bytes 6292042 | solution.py:28
  393.3 5.6 %fusion.3 = f32[1,1024,256]{2,1,0:T(8,128)S(1)} fusion(f32[2,1024,1024]{2,1,0:T(8,128)} %get-tuple-element.31, s32[]{:T(128)S(6)} %select_n.14, f32[16,256,1024]{2,1,0:T(8,128)} %get-tuple-element.33, s32[]{:T(128)} %bitcast.2), kind=kOutput, calls=%fused_computation.3 | convolution fusion | flops 3221225472 | bytes 6291972 | tf_op jit(solution)/shard_map/while/body/eval_jaxpr/cond/branch_1_fun/ak,bk->ab/dot_general | solution.py:10
  401.1 8.8 %conditional.2 = (f32[1,1024,256]{2,1,0:T(8,128)S(1)}) conditional(s32[]{:T(128)} %bitcast.18, () %tuple.35, (s32[1,2]{1,0:T(1,128)S(1)}, f32[2,1024,1024]{2,1,0:T(8,128)}, f32[16,256,1024]{2,1,0:T(8,128)}) %tuple.36), branch_computations={%region_1.1_spmd, %region_2.2_spmd} | conditional | flops 3221225472 | bytes 6292042 | solution.py:28
  404.3 5.6 %fusion.3 = f32[1,1024,256]{2,1,0:T(8,128)S(1)} fusion(f32[2,1024,1024]{2,1,0:T(8,128)} %get-tuple-element.31, s32[]{:T(128)S(6)} %select_n.14, f32[16,256,1024]{2,1,0:T(8,128)} %get-tuple-element.33, s32[]{:T(128)} %bitcast.2), kind=kOutput, calls=%fused_computation.3 | convolution fusion | flops 3221225472 | bytes 6291972 | tf_op jit(solution)/shard_map/while/body/eval_jaxpr/cond/branch_1_fun/ak,bk->ab/dot_general | solution.py:10
  412.0 8.8 %conditional.2 = (f32[1,1024,256]{2,1,0:T(8,128)S(1)}) conditional(s32[]{:T(128)} %bitcast.18, () %tuple.35, (s32[1,2]{1,0:T(1,128)S(1)}, f32[2,1024,1024]{2,1,0:T(8,128)}, f32[16,256,1024]{2,1,0:T(8,128)}) %tuple.36), branch_computations={%region_1.1_spmd, %region_2.2_spmd} | conditional | flops 3221225472 | bytes 6292042 | solution.py:28
  415.2 5.6 %fusion.3 = f32[1,1024,256]{2,1,0:T(8,128)S(1)} fusion(f32[2,1024,1024]{2,1,0:T(8,128)} %get-tuple-element.31, s32[]{:T(128)S(6)} %select_n.14, f32[16,256,1024]{2,1,0:T(8,128)} %get-tuple-element.33, s32[]{:T(128)} %bitcast.2), kind=kOutput, calls=%fused_computation.3 | convolution fusion | flops 3221225472 | bytes 6291972 | tf_op jit(solution)/shard_map/while/body/eval_jaxpr/cond/branch_1_fun/ak,bk->ab/dot_general | solution.py:10
  423.0 8.8 %conditional.2 = (f32[1,1024,256]{2,1,0:T(8,128)S(1)}) conditional(s32[]{:T(128)} %bitcast.18, () %tuple.35, (s32[1,2]{1,0:T(1,128)S(1)}, f32[2,1024,1024]{2,1,0:T(8,128)}, f32[16,256,1024]{2,1,0:T(8,128)}) %tuple.36), branch_computations={%region_1.1_spmd, %region_2.2_spmd} | conditional | flops 3221225472 | bytes 6292042 | solution.py:28
  426.2 5.6 %fusion.3 = f32[1,1024,256]{2,1,0:T(8,128)S(1)} fusion(f32[2,1024,1024]{2,1,0:T(8,128)} %get-tuple-element.31, s32[]{:T(128)S(6)} %select_n.14, f32[16,256,1024]{2,1,0:T(8,128)} %get-tuple-element.33, s32[]{:T(128)} %bitcast.2), kind=kOutput, calls=%fused_computation.3 | convolution fusion | flops 3221225472 | bytes 6291972 | tf_op jit(solution)/shard_map/while/body/eval_jaxpr/cond/branch_1_fun/ak,bk->ab/dot_general | solution.py:10
  433.9 8.8 %conditional.2 = (f32[1,1024,256]{2,1,0:T(8,128)S(1)}) conditional(s32[]{:T(128)} %bitcast.18, () %tuple.35, (s32[1,2]{1,0:T(1,128)S(1)}, f32[2,1024,1024]{2,1,0:T(8,128)}, f32[16,256,1024]{2,1,0:T(8,128)}) %tuple.36), branch_computations={%region_1.1_spmd, %region_2.2_spmd} | conditional | flops 3221225472 | bytes 6292042 | solution.py:28
  437.1 5.6 %fusion.3 = f32[1,1024,256]{2,1,0:T(8,128)S(1)} fusion(f32[2,1024,1024]{2,1,0:T(8,128)} %get-tuple-element.31, s32[]{:T(128)S(6)} %select_n.14, f32[16,256,1024]{2,1,0:T(8,128)} %get-tuple-element.33, s32[]{:T(128)} %bitcast.2), kind=kOutput, calls=%fused_computation.3 | convolution fusion | flops 3221225472 | bytes 6291972 | tf_op jit(solution)/shard_map/while/body/eval_jaxpr/cond/branch_1_fun/ak,bk->ab/dot_general | solution.py:10
  443.8 21.9 %sub.8 = f32[20,1024,256]{2,1,0:T(8,128)} subtract(f32[20,1024,256]{2,1,0:T(8,128)} %param.10, f32[20,1024,256]{2,1,0:T(8,128)} %get-tuple-element.43) | non-fusion elementwise | flops 5242880 | bytes 62914560 | tf_op jit(solution)/shard_map/sub | solution.py:35
  (92 shorter events, 38.9 us)
Async XLA Ops:
  7.2 49.6 %copy-start = (f32[2,256,1024]{2,1,0:T(8,128)S(1)}, f32[2,256,1024]{2,1,0:T(8,128)}, u32[]{:S(2)}) copy-start(f32[2,256,1024]{2,1,0:T(8,128)} %param.9) | copy-start | bytes 6291460
  7.2 49.6 %all-gather.3.cloned.1.call-start = ((), (), s32[]{:S(2)}) async-start(), calls=%async_computation | async-start | bytes 4718592 | tf_op jit(solution)/shard_map/all_gather | solution.py:14
  7.9 216.6 %all-gather.5.cloned.1.call-start = ((), (), s32[]{:S(2)}) async-start(), calls=%async_computation.1 | async-start | bytes 18874368 | tf_op jit(solution)/shard_map/all_gather | solution.py:24
  66.4 153.9 %copy-start.2 = (f32[2,256,1024]{2,1,0:T(8,128)S(1)}, f32[2,256,1024]{2,1,0:T(8,128)}, u32[]{:S(2)}) copy-start(f32[2,256,1024]{2,1,0:T(8,128)} %fusion.9) | copy-start | bytes 6291460
  66.4 48.2 %collective-permute-start = (f32[2,256,1024]{2,1,0:T(8,128)}, f32[2,256,1024]{2,1,0:T(8,128)S(1)}, u32[]{:S(2)}, u32[]{:S(2)}) collective-permute-start(f32[2,256,1024]{2,1,0:T(8,128)} %fusion.9), channel_id=1, source_target_pairs={{0,1},{1,2},{2,3},{3,0},{4,5},{5,6},{6,7},{7,4},{8,9},{9,10},{10,1... | collective-permute-start | bytes 6291464 | tf_op jit(solution)/shard_map/ppermute | solution.py:20
  114.6 1.3 copy-start.3
  116.0 47.2 %collective-permute-start.1 = (f32[2,256,1024]{2,1,0:T(8,128)S(1)}, f32[2,256,1024]{2,1,0:T(8,128)}, u32[]{:S(2)}, u32[]{:S(2)}) collective-permute-start(f32[2,256,1024]{2,1,0:T(8,128)S(1)} %collective-permute-done), channel_id=1, source_target_pairs={{0,1},{1,2},{2,3},{3,0},{4,5},{5,6},{6,7},{7,4},{8,9},{9,10},{10,1... | collective-permute-start | bytes 6291464 | tf_op jit(solution)/shard_map/ppermute | solution.py:20
  163.1 46.5 %collective-permute-start.2 = (f32[2,256,1024]{2,1,0:T(8,128)}, f32[2,256,1024]{2,1,0:T(8,128)}, u32[]{:S(2)}, u32[]{:S(2)}) collective-permute-start(f32[2,256,1024]{2,1,0:T(8,128)} %collective-permute-done.1), channel_id=1, source_target_pairs={{0,1},{1,2},{2,3},{3,0},{4,5},{5,6},{6,7},{7,4},{8,9},{9,10},{10,1... | collective-permute-start | bytes 6291464 | tf_op jit(solution)/shard_map/ppermute | solution.py:20
  163.9 56.1 %copy-start.4 = (f32[2,256,1024]{2,1,0:T(8,128)S(1)}, f32[2,256,1024]{2,1,0:T(8,128)}, u32[]{:S(2)}) copy-start(f32[2,256,1024]{2,1,0:T(8,128)} %copy-done.3) | copy-start | bytes 6291460
  443.8 21.9 %copy-start.1 = (f32[2,256,1024]{2,1,0:T(8,128)S(1)}, f32[2,256,1024]{2,1,0:T(8,128)}, u32[]{:S(2)}) copy-start(f32[2,256,1024]{2,1,0:T(8,128)} %param.9) | copy-start | bytes 6291460
Sparse Core Ops, SparseCore 0:
  9.6 47.1 all-gather.2
  66.6 149.2 all-gather.4
